TPU v7x, 32 devices: a whole 2x2x4 slice. The times are simulated.
32 devices in a mesh: ctx: 16 (over z, y, core), section: 2 (over x).
Axes of the slice: x: 2, y: 2, z: 4, core: 2. Of those that a mesh axis runs over, the one named last changes fastest.
Arguments:
- queries: bfloat16 [2, 2048, 2560], P('section', 'ctx'), may hold values from -80 to 80
- grad_out: bfloat16 [2, 2048, 2560], P('section', 'ctx'), may hold values from -6 to 6
- keys_values: bfloat16 [2, 2048, 512], P(None, 'ctx'), may hold values from -16 to 16
- doc_ids: int32 [2048], replicated, may hold values from 0 to 7, never falling along the last dimension, each value on 1 to 512 neighbouring positions
Outputs:
- grad_queries: bfloat16 [2, 2048, 2560], P('section', 'ctx')
- grad_kv: bfloat16 [2, 2048, 512], P(None, ('ctx', 'section'))
Inputs may be any that keep to these rules, and one draw needn't show every extreme that they name: `doc_ids`: document numbers never fall along the sequence; a document has at most 512 tokens.
All inputs are finite; a program needn't handle non-finite values.
Results may differ from a plain program's by a relative error of at most 0.015.
Values may be sent and summed in bfloat16 or wider, within the bound.
A program may use at most 64 MiB of HBM per device.

v0:
```python
import jax
import jax.numpy as jnp
from jax import lax
from jax.sharding import PartitionSpec as P

HD = 128


def from_behind(value, axis, steps):
    count = lax.axis_size(axis)
    first, last = (max(0, -steps), min(count, count - steps))
    return lax.ppermute(value, axis, [(source, source + steps) for source in range(first, last)])


def body(queries, grad_out, keys_values, doc_ids):
    layers, tok_rows, width = queries.shape
    kv_width = keys_values.shape[2]
    heads_kv = kv_width // HD
    group = width // kv_width
    scale = HD ** (-0.5)
    reach = lax.axis_size("ctx") // 4
    span = reach + 1
    pieces = [keys_values]
    for offset in range(1, reach + 1):
        pieces.append(from_behind(keys_values, "ctx", offset))
    whole = jnp.concatenate(pieces[::-1], axis=1)
    total = span * tok_rows
    keys = whole[0].reshape(total, heads_kv, HD)
    values = whole[1].reshape(total, heads_kv, HD)
    qrows = queries.reshape(layers, tok_rows, heads_kv, group, HD)
    grows = grad_out.reshape(layers, tok_rows, heads_kv, group, HD)
    first = lax.axis_index("ctx") * tok_rows
    qplace = first + jnp.arange(tok_rows, dtype=jnp.int32)
    qdoc = lax.dynamic_slice_in_dim(doc_ids, first, tok_rows, 0)
    padded_docs = jnp.concatenate([jnp.full((reach * tok_rows,), -1, jnp.int32), doc_ids])
    window_docs = lax.dynamic_slice_in_dim(padded_docs, first, total, 0)
    window_places = first - reach * tok_rows + jnp.arange(total, dtype=jnp.int32)
    shards = 1
    for count in range(1, span + 1):
        if span % count == 0 and count * tok_rows <= max(512, tok_rows):
            shards = count
    kblock = shards * tok_rows
    nblocks = span // shards

    def block_parts(index):
        start = index * kblock
        kplace = lax.dynamic_slice_in_dim(window_places, start, kblock, 0)
        kdoc = lax.dynamic_slice_in_dim(window_docs, start, kblock, 0)
        visible = (kplace[None, :] <= qplace[:, None]) & (kdoc[None, :] == qdoc[:, None])
        kpart = lax.dynamic_slice_in_dim(keys, start, kblock, 0)
        vpart = lax.dynamic_slice_in_dim(values, start, kblock, 0)
        return (visible, kpart, vpart)

    def block_scores(kpart, visible):
        scores = (
            jnp.einsum("ltgnd,kgd->ltgnk", qrows, kpart, preferred_element_type=jnp.float32) * scale
        )
        return jnp.where(visible[None, :, None, None, :], scores, -1e30)

    def forward_step(carry, index):
        visible, kpart, vpart = block_parts(index)

        def forward_compute(state):
            top, summed, accum = state
            seen = visible[None, :, None, None, :]
            scores = block_scores(kpart, visible)
            new_top = jnp.maximum(top, jnp.max(scores, axis=-1))
            factor = jnp.exp(top - new_top)
            weights = jnp.where(seen, jnp.exp(scores - new_top[..., None]), 0.0)
            summed = summed * factor + jnp.sum(weights, axis=-1)
            accum = accum * factor[..., None] + jnp.einsum(
                "ltgnk,kgd->ltgnd",
                weights,
                vpart.astype(jnp.float32),
                precision=lax.Precision.HIGHEST,
            )
            return (new_top, summed, accum)

        carry = lax.cond(jnp.any(visible), forward_compute, lambda state: state, carry)
        return (carry, None)

    stat_shape = (layers, tok_rows, heads_kv, group)
    start_state = (
        jnp.full(stat_shape, -1e30, jnp.float32),
        jnp.zeros(stat_shape, jnp.float32),
        jnp.zeros(stat_shape + (HD,), jnp.float32),
    )
    (top, summed, accum), unused = lax.scan(
        forward_step, start_state, jnp.arange(nblocks, dtype=jnp.int32)
    )
    lse = top + jnp.log(summed)
    delta = jnp.sum(grows.astype(jnp.float32) * (accum / summed[..., None]), axis=-1)

    def backward_step(dquery, index):
        visible, kpart, vpart = block_parts(index)

        def backward_compute(dquery):
            seen = visible[None, :, None, None, :]
            scores = block_scores(kpart, visible)
            prob = jnp.where(seen, jnp.exp(scores - lse[..., None]), 0.0).astype(jnp.bfloat16)
            dprob = jnp.einsum("ltgnd,kgd->ltgnk", grows, vpart, preferred_element_type=jnp.float32)
            dscore = (prob.astype(jnp.float32) * (dprob - delta[..., None])).astype(jnp.bfloat16)
            dquery = dquery + scale * jnp.einsum(
                "ltgnk,kgd->ltgnd", dscore, kpart, preferred_element_type=jnp.float32
            )
            dkeys = scale * jnp.einsum(
                "ltgnk,ltgnd->kgd", dscore, qrows, preferred_element_type=jnp.float32
            )
            dvalues = jnp.einsum(
                "ltgnk,ltgnd->kgd", prob, grows, preferred_element_type=jnp.float32
            )
            return (dquery, (dkeys, dvalues))

        def skipped(dquery):
            empty = jnp.zeros((kblock, heads_kv, HD), jnp.float32)
            return (dquery, (empty, empty))

        return lax.cond(jnp.any(visible), backward_compute, skipped, dquery)

    dquery, (dkeys, dvalues) = lax.scan(
        backward_step,
        jnp.zeros(stat_shape + (HD,), jnp.float32),
        jnp.arange(nblocks, dtype=jnp.int32),
    )
    grad_queries = dquery.reshape(layers, tok_rows, width).astype(jnp.bfloat16)
    grads = jnp.stack([dkeys.reshape(total, kv_width), dvalues.reshape(total, kv_width)]).reshape(
        2, span, tok_rows, kv_width
    )
    collected = grads[:, reach]
    for offset in range(1, reach + 1):
        collected = collected + from_behind(
            grads[:, reach - offset].astype(jnp.bfloat16), "ctx", -offset
        ).astype(jnp.float32)
    gathered = lax.psum_scatter(
        collected.astype(jnp.bfloat16), "section", scatter_dimension=1, tiled=True
    )
    return (grad_queries, gathered)


def solution(mesh):
    return jax.shard_map(
        body,
        mesh=mesh,
        in_specs=(P("section", "ctx", None), P("section", "ctx", None), P(None, "ctx", None), P()),
        out_specs=(P("section", "ctx", None), P(None, ("ctx", "section"), None)),
        check_vma=False,
    )
```

profile of v0, /device:TPU:13, one launch (start us, length us, event | category | flops | bytes accessed | tf_op | source)
XLA Modules:
  0.0 161.2 jit_solution(5687547614020313144)
XLA Ops:
  8.3 3.2 %collective-permute-start = (bf16[2,128,512]{1,2,0:T(8,128)(2,1)S(1)}, bf16[2,128,512]{1,2,0:T(8,128)(2,1)}, u32[]{:S(2)}, u32[]{:S(2)}) collective-permute-start(bf16[2,128,512]{1,2,0:T(8,128)(2,1)S(1)} %copy.17), channel_id=1, source_target_pairs={{0,8},{2,10},{4,12},{6,14},{8,16},{10,18},{12,20},{14,22},{16,24},... | collective-permute-start | bytes 786440 | tf_op jit(solution)/shard_map/ppermute | solution.py:12
  11.5 4.0 %collective-permute-start.1 = (bf16[2,128,512]{1,2,0:T(8,128)(2,1)S(1)}, bf16[2,128,512]{1,2,0:T(8,128)(2,1)S(1)}, u32[]{:S(2)}, u32[]{:S(2)}) collective-permute-start(bf16[2,128,512]{1,2,0:T(8,128)(2,1)S(1)} %copy.17), channel_id=1, source_target_pairs={{0,6},{2,8},{4,10},{6,12},{8,14},{10,16},{12,18},{14,20},{16,22},{... | collective-permute-start | bytes 786440 | tf_op jit(solution)/shard_map/ppermute | solution.py:12
  15.6 2.5 %collective-permute-start.3 = (bf16[2,128,512]{1,2,0:T(8,128)(2,1)S(1)}, bf16[2,128,512]{1,2,0:T(8,128)(2,1)S(1)}, u32[]{:S(2)}, u32[]{:S(2)}) collective-permute-start(bf16[2,128,512]{1,2,0:T(8,128)(2,1)S(1)} %copy.17), channel_id=1, source_target_pairs={{0,2},{2,4},{4,6},{6,8},{8,10},{10,12},{12,14},{14,16},{16,18},{18... | collective-permute-start | bytes 786440 | tf_op jit(solution)/shard_map/ppermute | solution.py:12
  18.1 2.5 %collective-permute-start.2 = (bf16[2,128,512]{1,2,0:T(8,128)(2,1)S(1)}, bf16[2,128,512]{1,2,0:T(8,128)(2,1)}, u32[]{:S(2)}, u32[]{:S(2)}) collective-permute-start(bf16[2,128,512]{1,2,0:T(8,128)(2,1)S(1)} %copy.17), channel_id=1, source_target_pairs={{0,4},{2,6},{4,8},{6,10},{8,12},{10,14},{12,16},{14,18},{16,20},{1... | collective-permute-start | bytes 786440 | tf_op jit(solution)/shard_map/ppermute | solution.py:12
  22.2 1.5 copy.22
  25.8 5.9 %collective-permute-done.2 = bf16[2,128,512]{1,2,0:T(8,128)(2,1)} collective-permute-done((bf16[2,128,512]{1,2,0:T(8,128)(2,1)S(1)}, bf16[2,128,512]{1,2,0:T(8,128)(2,1)}, u32[]{:S(2)}, u32[]{:S(2)}) %collective-permute-start.2) | collective-permute-done | bytes 262176 | tf_op jit(solution)/shard_map/ppermute | solution.py:12
  35.3 26.5 %while.33 = (s32[]{:T(128)}, f32[1,128,4,5]{1,3,2,0:T(8,128)S(1)}, f32[1,128,4,5]{1,3,2,0:T(8,128)S(1)}, f32[1,128,4,5,128]{1,4,3,2,0:T(8,128)S(1)}, s32[5]{0:T(...) while((s32[]{:T(128)}, f32[1,128,4,5]{1,3,2,0:T(8,128)S(1)}, ...), condition=%wide.region_6.7_spmd.clone, body=%wide.region_0.6_spmd.clone.sunk | while | flops 590552704 | bytes 7718245 | solution.py:88
  40.8 3.2 %conditional.6 = ((f32[1,128,4,5]{1,3,2,0:T(8,128)S(1)}, f32[1,128,4,5]{1,3,2,0:T(8,128)S(1)}, f32[1,128,4,5,128]{1,4,3,2,0:T(8,128)S(1)})) conditional(s32[]{:T(128)} %convert_element_type.107, (f32[1,128,4,5]{1,3,2,0:T(8,128)S(1)}, f32[1,128,4,5]{1,3,2,0:T(8,128)S(1)}, f32[1,128,4,5,128]{1,4,3,2,0:T(8,128)S(1)}) %tuple.91, ...), branch_computations={%region_2.2_spmd, %region_3.5_spmd} | conditional | flops 590487040 | bytes 7696932 | solution.py:79
  42.4 1.5 fusion.5
  46.7 3.2 %conditional.6 = ((f32[1,128,4,5]{1,3,2,0:T(8,128)S(1)}, f32[1,128,4,5]{1,3,2,0:T(8,128)S(1)}, f32[1,128,4,5,128]{1,4,3,2,0:T(8,128)S(1)})) conditional(s32[]{:T(128)} %convert_element_type.107, (f32[1,128,4,5]{1,3,2,0:T(8,128)S(1)}, f32[1,128,4,5]{1,3,2,0:T(8,128)S(1)}, f32[1,128,4,5,128]{1,4,3,2,0:T(8,128)S(1)}) %tuple.91, ...), branch_computations={%region_2.2_spmd, %region_3.5_spmd} | conditional | flops 590487040 | bytes 7696932 | solution.py:79
  48.3 1.6 fusion.5
  52.6 3.2 %conditional.6 = ((f32[1,128,4,5]{1,3,2,0:T(8,128)S(1)}, f32[1,128,4,5]{1,3,2,0:T(8,128)S(1)}, f32[1,128,4,5,128]{1,4,3,2,0:T(8,128)S(1)})) conditional(s32[]{:T(128)} %convert_element_type.107, (f32[1,128,4,5]{1,3,2,0:T(8,128)S(1)}, f32[1,128,4,5]{1,3,2,0:T(8,128)S(1)}, f32[1,128,4,5,128]{1,4,3,2,0:T(8,128)S(1)}) %tuple.91, ...), branch_computations={%region_2.2_spmd, %region_3.5_spmd} | conditional | flops 590487040 | bytes 7696932 | solution.py:79
  54.2 1.6 fusion.5
  58.6 3.2 %conditional.6 = ((f32[1,128,4,5]{1,3,2,0:T(8,128)S(1)}, f32[1,128,4,5]{1,3,2,0:T(8,128)S(1)}, f32[1,128,4,5,128]{1,4,3,2,0:T(8,128)S(1)})) conditional(s32[]{:T(128)} %convert_element_type.107, (f32[1,128,4,5]{1,3,2,0:T(8,128)S(1)}, f32[1,128,4,5]{1,3,2,0:T(8,128)S(1)}, f32[1,128,4,5,128]{1,4,3,2,0:T(8,128)S(1)}) %tuple.91, ...), branch_computations={%region_2.2_spmd, %region_3.5_spmd} | conditional | flops 590487040 | bytes 7696932 | solution.py:79
  60.2 1.5 fusion.5
  63.2 39.4 %while.34 = (s32[]{:T(128)}, f32[1,128,4,5,128]{1,4,3,2,0:T(8,128)S(1)}, f32[5,128,4,128]{3,2,1,0:T(4,128)}, f32[5,128,4,128]{3,2,1,0:T(4,128)}, s32[5]{0:T(128)...) while((s32[]{:T(128)}, ...), condition=%wide.region_12.13_spmd.clone, body=%wide.region_8.12_spmd.clone.sunk | while | flops 423166080 | bytes 11200869 | solution.py:120
  70.1 4.9 %conditional.7 = (f32[1,128,4,5,128]{1,4,3,2,0:T(8,128)S(1)}, f32[1,128,4,128]{3,1,2,0:T(8,128)S(1)}, f32[1,128,4,128]{3,1,2,0:T(8,128)S(1)}) conditional(s32[]{:T(128)} %convert_element_type.108, f32[1,128,4,5,128]{1,4,3,2,0:T(8,128)S(1)} %get-tuple-element.750, (bf16[640,4,128]{2,0,1:T(8,128)(2,1)}, s32[]{:T(128)}, ...), branch_computations={%region_10.10_spmd, %region_11.11_spmd} | conditional | flops 423100416 | bytes 10130968 | solution.py:118
  78.9 4.9 %conditional.7 = (f32[1,128,4,5,128]{1,4,3,2,0:T(8,128)S(1)}, f32[1,128,4,128]{3,1,2,0:T(8,128)S(1)}, f32[1,128,4,128]{3,1,2,0:T(8,128)S(1)}) conditional(s32[]{:T(128)} %convert_element_type.108, f32[1,128,4,5,128]{1,4,3,2,0:T(8,128)S(1)} %get-tuple-element.750, (bf16[640,4,128]{2,0,1:T(8,128)(2,1)}, s32[]{:T(128)}, ...), branch_computations={%region_10.10_spmd, %region_11.11_spmd} | conditional | flops 423100416 | bytes 10130968 | solution.py:118
  79.0 1.4 select_convert_fusion
  87.8 4.9 %conditional.7 = (f32[1,128,4,5,128]{1,4,3,2,0:T(8,128)S(1)}, f32[1,128,4,128]{3,1,2,0:T(8,128)S(1)}, f32[1,128,4,128]{3,1,2,0:T(8,128)S(1)}) conditional(s32[]{:T(128)} %convert_element_type.108, f32[1,128,4,5,128]{1,4,3,2,0:T(8,128)S(1)} %get-tuple-element.750, (bf16[640,4,128]{2,0,1:T(8,128)(2,1)}, s32[]{:T(128)}, ...), branch_computations={%region_10.10_spmd, %region_11.11_spmd} | conditional | flops 423100416 | bytes 10130968 | solution.py:118
  87.8 1.4 select_convert_fusion
  96.6 4.9 %conditional.7 = (f32[1,128,4,5,128]{1,4,3,2,0:T(8,128)S(1)}, f32[1,128,4,128]{3,1,2,0:T(8,128)S(1)}, f32[1,128,4,128]{3,1,2,0:T(8,128)S(1)}) conditional(s32[]{:T(128)} %convert_element_type.108, f32[1,128,4,5,128]{1,4,3,2,0:T(8,128)S(1)} %get-tuple-element.750, (bf16[640,4,128]{2,0,1:T(8,128)(2,1)}, s32[]{:T(128)}, ...), branch_computations={%region_10.10_spmd, %region_11.11_spmd} | conditional | flops 423100416 | bytes 10130968 | solution.py:118
  102.7 1.8 %stack.8 = f32[1,5,128,512]{3,2,0,1:T(8,128)S(1)} reshape(f32[5,128,4,128]{3,2,1,0:T(4,128)} %get-tuple-element.302) | data formatting | bytes 2621440 | tf_op jit(solution)/shard_map/stack | solution.py:126
  104.5 2.7 %stack.7 = f32[1,5,128,512]{3,2,0,1:T(8,128)} reshape(f32[5,128,4,128]{3,2,1,0:T(4,128)} %get-tuple-element.301) | data formatting | bytes 2621440 | tf_op jit(solution)/shard_map/stack | solution.py:126
  109.0 1.9 %collective-permute-start.4 = (bf16[2,128,512]{2,1,0:T(8,128)(2,1)S(1)}, bf16[2,128,512]{2,1,0:T(8,128)(2,1)S(1)}, u32[]{:S(2)}, u32[]{:S(2)}) collective-permute-start(bf16[2,128,512]{2,1,0:T(8,128)(2,1)S(1)} %get-tuple-element.474), channel_id=1, source_target_pairs={{2,0},{4,2},{6,4},{8,6},{10,8},{12,10},{14,12},{16,14},{18,16},{20... | collective-permute-start | bytes 786440 | tf_op jit(solution)/shard_map/ppermute | solution.py:12
  110.9 1.9 %collective-permute-start.7 = (bf16[2,128,512]{2,1,0:T(8,128)(2,1)S(1)}, bf16[2,128,512]{2,1,0:T(8,128)(2,1)S(1)}, u32[]{:S(2)}, u32[]{:S(2)}) collective-permute-start(bf16[2,128,512]{2,1,0:T(8,128)(2,1)S(1)} %get-tuple-element.475), channel_id=1, source_target_pairs={{8,0},{10,2},{12,4},{14,6},{16,8},{18,10},{20,12},{22,14},{24,16},... | collective-permute-start | bytes 786440 | tf_op jit(solution)/shard_map/ppermute | solution.py:12
  112.8 2.7 %collective-permute-start.6 = (bf16[2,128,512]{2,1,0:T(8,128)(2,1)S(1)}, bf16[2,128,512]{2,1,0:T(8,128)(2,1)S(1)}, u32[]{:S(2)}, u32[]{:S(2)}) collective-permute-start(bf16[2,128,512]{2,1,0:T(8,128)(2,1)S(1)} %get-tuple-element.476), channel_id=1, source_target_pairs={{6,0},{8,2},{10,4},{12,6},{14,8},{16,10},{18,12},{20,14},{22,16},{... | collective-permute-start | bytes 786440 | tf_op jit(solution)/shard_map/ppermute | solution.py:12
  115.6 2.0 %collective-permute-start.5 = (bf16[2,128,512]{2,1,0:T(8,128)(2,1)S(1)}, bf16[2,128,512]{2,1,0:T(8,128)(2,1)S(1)}, u32[]{:S(2)}, u32[]{:S(2)}) collective-permute-start(bf16[2,128,512]{2,1,0:T(8,128)(2,1)S(1)} %get-tuple-element.477), channel_id=1, source_target_pairs={{4,0},{6,2},{8,4},{10,6},{12,8},{14,10},{16,12},{18,14},{20,16},{2... | collective-permute-start | bytes 786440 | tf_op jit(solution)/shard_map/ppermute | solution.py:12
  117.6 1.7 %collective-permute-done.4 = bf16[2,128,512]{2,1,0:T(8,128)(2,1)S(1)} collective-permute-done((bf16[2,128,512]{2,1,0:T(8,128)(2,1)S(1)}, bf16[2,128,512]{2,1,0:T(8,128)(2,1)S(1)}, u32[]{:S(2)}, u32[]{:S(2)}) %collective-permute-start.4) | collective-permute-done | bytes 262176 | tf_op jit(solution)/shard_map/ppermute | solution.py:12
  119.3 1.5 collective-permute-done.6
  120.8 12.1 %collective-permute-done.5 = bf16[2,128,512]{2,1,0:T(8,128)(2,1)S(1)} collective-permute-done((bf16[2,128,512]{2,1,0:T(8,128)(2,1)S(1)}, bf16[2,128,512]{2,1,0:T(8,128)(2,1)S(1)}, u32[]{:S(2)}, u32[]{:S(2)}) %collective-permute-start.5) | collective-permute-done | bytes 262176 | tf_op jit(solution)/shard_map/ppermute | solution.py:12
  135.1 19.3 %reduce-scatter.2.cloned.1.call-done = bf16[2,64,512]{2,1,0:T(8,128)(2,1)} async-done(((bf16[2,128,512]{2,1,0:T(8,128)(2,1)}), bf16[2,64,512]{2,1,0:T(8,128)(2,1)}) %reduce-scatter.2.cloned.1.call-update) | async-done | bytes 131088 | tf_op jit(solution)/shard_map/reduce_scatter | solution.py:134
  (138 shorter events, 57.4 us)
Async XLA Ops:
  7.2 147.2 %reduce-scatter.2.cloned.1.call-start = ((), (), s32[]{:S(2)}) async-start(), calls=%async_computation.1 | async-start | bytes 393216 | tf_op jit(solution)/shard_map/reduce_scatter | solution.py:134
  8.3 16.4 %collective-permute-start = (bf16[2,128,512]{1,2,0:T(8,128)(2,1)S(1)}, bf16[2,128,512]{1,2,0:T(8,128)(2,1)}, u32[]{:S(2)}, u32[]{:S(2)}) collective-permute-start(bf16[2,128,512]{1,2,0:T(8,128)(2,1)S(1)} %copy.17), channel_id=1, source_target_pairs={{0,8},{2,10},{4,12},{6,14},{8,16},{10,18},{12,20},{14,22},{16,24},... | collective-permute-start | bytes 786440 | tf_op jit(solution)/shard_map/ppermute | solution.py:12
  11.5 14.1 %collective-permute-start.1 = (bf16[2,128,512]{1,2,0:T(8,128)(2,1)S(1)}, bf16[2,128,512]{1,2,0:T(8,128)(2,1)S(1)}, u32[]{:S(2)}, u32[]{:S(2)}) collective-permute-start(bf16[2,128,512]{1,2,0:T(8,128)(2,1)S(1)} %copy.17), channel_id=1, source_target_pairs={{0,6},{2,8},{4,10},{6,12},{8,14},{10,16},{12,18},{14,20},{16,22},{... | collective-permute-start | bytes 786440 | tf_op jit(solution)/shard_map/ppermute | solution.py:12
  15.6 17.1 %collective-permute-start.3 = (bf16[2,128,512]{1,2,0:T(8,128)(2,1)S(1)}, bf16[2,128,512]{1,2,0:T(8,128)(2,1)S(1)}, u32[]{:S(2)}, u32[]{:S(2)}) collective-permute-start(bf16[2,128,512]{1,2,0:T(8,128)(2,1)S(1)} %copy.17), channel_id=1, source_target_pairs={{0,2},{2,4},{4,6},{6,8},{8,10},{10,12},{12,14},{14,16},{16,18},{18... | collective-permute-start | bytes 786440 | tf_op jit(solution)/shard_map/ppermute | solution.py:12
  18.1 13.6 %collective-permute-start.2 = (bf16[2,128,512]{1,2,0:T(8,128)(2,1)S(1)}, bf16[2,128,512]{1,2,0:T(8,128)(2,1)}, u32[]{:S(2)}, u32[]{:S(2)}) collective-permute-start(bf16[2,128,512]{1,2,0:T(8,128)(2,1)S(1)} %copy.17), channel_id=1, source_target_pairs={{0,4},{2,6},{4,8},{6,10},{8,12},{10,14},{12,16},{14,18},{16,20},{1... | collective-permute-start | bytes 786440 | tf_op jit(solution)/shard_map/ppermute | solution.py:12
  22.2 1.8 %copy-start.1 = (bf16[1,128,2560]{2,1,0:T(8,128)(2,1)S(1)}, bf16[1,128,2560]{2,1,0:T(8,128)(2,1)}, u32[]{:S(2)}) copy-start(bf16[1,128,2560]{2,1,0:T(8,128)(2,1)} %param.13) | copy-start | bytes 1966084
  24.3 8.4 %copy-start = (bf16[1,128,2560]{1,2,0:T(8,128)(2,1)}, bf16[1,128,2560]{1,2,0:T(8,128)(2,1)S(1)}, u32[]{:S(2)}) copy-start(bf16[1,128,2560]{1,2,0:T(8,128)(2,1)S(1)} %copy.25) | copy-start | bytes 1966084
  109.0 10.3 %collective-permute-start.4 = (bf16[2,128,512]{2,1,0:T(8,128)(2,1)S(1)}, bf16[2,128,512]{2,1,0:T(8,128)(2,1)S(1)}, u32[]{:S(2)}, u32[]{:S(2)}) collective-permute-start(bf16[2,128,512]{2,1,0:T(8,128)(2,1)S(1)} %get-tuple-element.474), channel_id=1, source_target_pairs={{2,0},{4,2},{6,4},{8,6},{10,8},{12,10},{14,12},{16,14},{18,16},{20... | collective-permute-start | bytes 786440 | tf_op jit(solution)/shard_map/ppermute | solution.py:12
  110.9 8.4 %collective-permute-start.7 = (bf16[2,128,512]{2,1,0:T(8,128)(2,1)S(1)}, bf16[2,128,512]{2,1,0:T(8,128)(2,1)S(1)}, u32[]{:S(2)}, u32[]{:S(2)}) collective-permute-start(bf16[2,128,512]{2,1,0:T(8,128)(2,1)S(1)} %get-tuple-element.475), channel_id=1, source_target_pairs={{8,0},{10,2},{12,4},{14,6},{16,8},{18,10},{20,12},{22,14},{24,16},... | collective-permute-start | bytes 786440 | tf_op jit(solution)/shard_map/ppermute | solution.py:12
  112.8 8.0 %collective-permute-start.6 = (bf16[2,128,512]{2,1,0:T(8,128)(2,1)S(1)}, bf16[2,128,512]{2,1,0:T(8,128)(2,1)S(1)}, u32[]{:S(2)}, u32[]{:S(2)}) collective-permute-start(bf16[2,128,512]{2,1,0:T(8,128)(2,1)S(1)} %get-tuple-element.476), channel_id=1, source_target_pairs={{6,0},{8,2},{10,4},{12,6},{14,8},{16,10},{18,12},{20,14},{22,16},{... | collective-permute-start | bytes 786440 | tf_op jit(solution)/shard_map/ppermute | solution.py:12
  115.6 17.4 %collective-permute-start.5 = (bf16[2,128,512]{2,1,0:T(8,128)(2,1)S(1)}, bf16[2,128,512]{2,1,0:T(8,128)(2,1)S(1)}, u32[]{:S(2)}, u32[]{:S(2)}) collective-permute-start(bf16[2,128,512]{2,1,0:T(8,128)(2,1)S(1)} %get-tuple-element.477), channel_id=1, source_target_pairs={{4,0},{6,2},{8,4},{10,6},{12,8},{14,10},{16,12},{18,14},{20,16},{2... | collective-permute-start | bytes 786440 | tf_op jit(solution)/shard_map/ppermute | solution.py:12
Sparse Core Ops, SparseCore 0:
  134.0 20.2 reduce-scatter.1
where the time goes:
time: 162 us; the launch traced here: 161 us
  waiting for transfers between devices  40.6 us (25%)
  matrix products  30.7 us (19%)
  local copies, waits for them, and re-layouts  29.5 us (18%)
  starting transfers between devices  20.9 us (13%)
  between operations  14.3 us (9%)
  loops' own time  13.1 us (8%)
  other arithmetic  12.1 us (7%)
    ppermute x8, waiting for transfers between devices, from_behind(): lax.ppermute(value, axis, [(source, source + steps) for source in range(f...  21.3 us
    ppermute x8, starting transfers between devices, from_behind(): lax.ppermute(value, axis, [(source, source + steps) for source in range(f...  20.8 us
    reduce_scatter x1, waiting for transfers between devices, body(): lax.psum_scatter(collected.astype(jnp.bfloat16), 'section', scatter_dimen...  19.3 us
    dot_general x8, matrix products, block_scores(): jnp.einsum('ltgnd,kgd->ltgnk', qrows, kpart, preferred_element_type=jnp.f...  11 us
    unnamed x17, local copies, waits for them, and re-layouts  10.4 us
    another operation x1, loops' own time, body(): lax.scan(backward_step, jnp.zeros(stat_shape + (HD,), jnp.float32), jnp.a...  6.39 us
    dot_general x4, matrix products, forward_compute(): jnp.einsum('ltgnk,kgd->ltgnd', weights, vpart.astype(jnp.float32), precis...  6.2 us
    another operation x1, loops' own time, body(): lax.scan(forward_step, start_state, jnp.arange(nblocks, dtype=jnp.int32))  6.2 us
  transfers between devices with their start and end apart: 9, of which 5 were waited for; matrix products, arithmetic and copies ran while one was open for 5% of the time, Pallas kernels for 0%

commit v1 on v0

v1 whole, which is shorter than its diff:
```python
import functools

import jax
import jax.numpy as jnp
from jax import lax
from jax.experimental import pallas as pl
from jax.experimental.pallas import tpu as pltpu
from jax.sharding import PartitionSpec as P

HD = 128
MESH = pl.DeviceIdType.MESH
LOG2E = 1.4426950408889634
NEG = -1e30


def kernel(
    n, sections, reach, heads_kv, group,
    q_ref, do_ref, kv_ref, docs_ref,
    dq_ref, out_ref,
    qbuf, dobuf, kvbuf, bias, pbuf, dsbuf, acc, sbuf, rbuf, dqbuf,
    lsem, qsend, qrecv, kvsend, kvrecv, gsend, grecv, dqsend, dqrecv, dqloc,
):
    me = lax.axis_index("ctx")
    sec = lax.axis_index("section")
    layers, rows = q_ref.shape[0], q_ref.shape[1]
    core = lax.rem(me, 2)
    other = 1 - core
    chip = me // 2
    chips = n // 2
    depth = reach // 2
    blocks = reach + 2
    heads = heads_kv // 2
    gw = group * HD
    window = (reach + 1) * rows
    piece = rows // sections
    scale = HD ** (-0.5)

    def dev(ctx, section):
        return {"ctx": ctx, "section": section}

    def cols(head, width):
        return pl.ds(pl.multiple_of(head * width, HD), width)

    def local_copies(h):
        g = core * heads + h
        return [
            pltpu.make_async_copy(q_ref.at[:, :, cols(g, gw)], qbuf.at[h, core], lsem.at[h, 0]),
            pltpu.make_async_copy(do_ref.at[:, :, cols(g, gw)], dobuf.at[h, core], lsem.at[h, 1]),
            pltpu.make_async_copy(
                kv_ref.at[:, :, cols(g, HD)], kvbuf.at[h, :, reach + core], lsem.at[h, 2]
            ),
        ]

    def q_copies(h):
        g = other * heads + h
        partner = dev(2 * chip + other, sec)
        return [
            pltpu.make_async_remote_copy(
                src_ref=src.at[:, :, cols(g, gw)], dst_ref=dst.at[h, core],
                send_sem=qsend.at[h, k], recv_sem=qrecv.at[h, k],
                device_id=partner, device_id_type=MESH,
            )
            for k, (src, dst) in enumerate([(q_ref, qbuf), (do_ref, dobuf)])
        ]

    def kv_copy(h, d, w):
        to = lax.rem(core + w, 2)
        slot = core - 2 * d + reach
        return pltpu.make_async_remote_copy(
            src_ref=kv_ref.at[:, :, cols(to * heads + h, HD)], dst_ref=kvbuf.at[h, :, slot],
            send_sem=kvsend.at[h, d, w], recv_sem=kvrecv.at[h, slot],
            device_id=dev(2 * (chip + d) + to, sec), device_id_type=MESH,
        )

    def kv_wait(h, slot):
        return pltpu.make_async_remote_copy(
            src_ref=kv_ref.at[:, :, pl.ds(0, HD)], dst_ref=kvbuf.at[h, :, slot],
            send_sem=kvsend.at[h, 0, 0], recv_sem=kvrecv.at[h, slot],
            device_id=dev(2 * chip + other, sec), device_id_type=MESH,
        )

    def g_copy(h, slot, t):
        d = (reach + 1 - slot) // 2
        owner_core = (slot - reach) % 2
        to = lax.rem(sec + t, sections)
        return pltpu.make_async_remote_copy(
            src_ref=sbuf.at[h, slot, :, pl.ds(pl.multiple_of(to * piece, piece), piece)],
            dst_ref=rbuf.at[d, sec, core, h],
            send_sem=gsend.at[h, slot, t], recv_sem=grecv.at[d, sec, core, h],
            device_id=dev(2 * (chip - d) + owner_core, to), device_id_type=MESH,
        )

    def g_wait(h, d, s, c):
        return pltpu.make_async_remote_copy(
            src_ref=sbuf.at[h, 0, :, pl.ds(0, piece)], dst_ref=rbuf.at[d, s, c, h],
            send_sem=gsend.at[h, 0, 0], recv_sem=grecv.at[d, s, c, h],
            device_id=dev(2 * chip + other, sec), device_id_type=MESH,
        )

    def dq_copy(h):
        return pltpu.make_async_remote_copy(
            src_ref=dqbuf.at[h, other], dst_ref=dq_ref.at[:, :, cols(core * heads + h, gw)],
            send_sem=dqsend.at[h], recv_sem=dqrecv.at[h],
            device_id=dev(2 * chip + other, sec), device_id_type=MESH,
        )

    def dq_wait(h):
        return pltpu.make_async_remote_copy(
            src_ref=dqbuf.at[h, other], dst_ref=dq_ref.at[:, :, cols(other * heads + h, gw)],
            send_sem=dqsend.at[h], recv_sem=dqrecv.at[h],
            device_id=dev(2 * chip + other, sec), device_id_type=MESH,
        )

    def dq_local(h):
        return pltpu.make_async_copy(
            dqbuf.at[h, core], dq_ref.at[:, :, cols(core * heads + h, gw)], dqloc.at[h]
        )

    barrier = pltpu.get_barrier_semaphore()
    for step in range(-depth, depth + 1):
        @pl.when((chip + step >= 0) & (chip + step < chips))
        def _():
            for w in range(2):
                for t in range(sections):
                    if step == 0 and w == 0 and t == 0:
                        continue
                    pl.semaphore_signal(
                        barrier, inc=1,
                        device_id=dev(2 * (chip + step) + lax.rem(core + w, 2), lax.rem(sec + t, sections)),
                        device_id_type=MESH,
                    )

    for h in range(heads):
        for copy in local_copies(h):
            copy.start()

    near = jnp.minimum(chip, depth) + jnp.minimum(chips - 1 - chip, depth) + 1
    pl.semaphore_wait(barrier, near * (2 * sections) - 1)

    for h in range(heads):
        for d in range(depth, 0, -1):
            @pl.when(chip + d < chips)
            def _():
                for w in range(2):
                    kv_copy(h, d, w).start()
        kv_copy(h, 0, 1).start()
        for copy in q_copies(h):
            copy.start()

    for d in range(1, depth + 1):
        @pl.when(chip - d < 0)
        def _():
            for slot in (reach - 2 * d, reach - 2 * d + 1):
                for h in range(heads):
                    kvbuf[h, :, slot] = jnp.zeros((2, rows, HD), jnp.bfloat16)

        @pl.when(chip + d >= chips)
        def _():
            rbuf[d] = jnp.zeros(rbuf.shape[1:], jnp.bfloat16)

    row_at = lax.broadcasted_iota(jnp.int32, (rows, rows), 0)
    col_at = lax.broadcasted_iota(jnp.int32, (rows, rows), 1)
    for slot in range(blocks):
        at = 2 * chip - reach + slot
        kdoc = docs_ref[pl.ds(jnp.maximum(at, 0), 1), :].astype(jnp.float32)
        kdoc = jnp.transpose(jnp.broadcast_to(kdoc, (rows, rows)))
        for sub in range(2):
            if not 0 <= slot - sub <= reach:
                continue
            qdoc = docs_ref[pl.ds(2 * chip + sub, 1), :].astype(jnp.float32)
            kplace = at * rows + row_at
            qplace = (2 * chip + sub) * rows + col_at
            seen = (kplace <= qplace) & (kplace >= 0) & (kdoc == qdoc)
            bias[sub, (slot - sub) * rows : (slot - sub + 1) * rows] = jnp.where(seen, 0.0, NEG)

    def head_step(h, unused):
        local_copies(h)[2].wait()
        for slot in range(blocks):
            at = 2 * chip - reach + slot
            if slot < reach:
                condition = at >= 0
            else:
                condition = core != slot - reach

            @pl.when(condition)
            def _():
                kv_wait(h, slot).wait_recv()

        acc[...] = jnp.zeros_like(acc)

        def sub_step(w, unused):
            sub = lax.rem(core + w, 2)

            @pl.when(w == 0)
            def _():
                for copy in local_copies(h)[:2]:
                    copy.wait()

            @pl.when(w == 1)
            def _():
                for copy in q_copies(h):
                    copy.wait_recv()

            k = kvbuf[h, 0, pl.ds(sub, reach + 1)].reshape(window, HD)
            v = kvbuf[h, 1, pl.ds(sub, reach + 1)].reshape(window, HD)
            kt = jnp.transpose(k)
            keys_at = pl.ds(pl.multiple_of(sub * rows, rows), window)
            for layer in range(layers):
                for i in range(group):
                    at = pl.ds(i * HD, HD)
                    q = qbuf[h, sub, layer, :, at]
                    do = dobuf[h, sub, layer, :, at]
                    nt = (((1,), (1,)), ((), ()))
                    s = lax.dot_general(k, q, nt, preferred_element_type=jnp.float32)
                    dp = lax.dot_general(v, do, nt, preferred_element_type=jnp.float32)
                    s = s * (scale * LOG2E) + bias[sub]
                    e = jnp.exp2(s - jnp.max(s, axis=0, keepdims=True))
                    inverse = 1.0 / jnp.sum(e, axis=0, keepdims=True)
                    delta = jnp.sum(e * dp, axis=0, keepdims=True) * inverse
                    p = (e * inverse).astype(jnp.bfloat16)
                    pbuf[:, i * rows : (i + 1) * rows] = p
                    dsbuf[:, i * rows : (i + 1) * rows] = (
                        p.astype(jnp.float32) * (dp - delta)
                    ).astype(jnp.bfloat16)
                stack_q = jnp.concatenate(
                    [qbuf[h, sub, layer, :, i * HD : (i + 1) * HD] for i in range(group)], axis=0
                )
                stack_do = jnp.concatenate(
                    [dobuf[h, sub, layer, :, i * HD : (i + 1) * HD] for i in range(group)], axis=0
                )
                acc[0, keys_at] += jnp.dot(dsbuf[...], stack_q, preferred_element_type=jnp.float32)
                acc[1, keys_at] += jnp.dot(pbuf[...], stack_do, preferred_element_type=jnp.float32)
                dqt = jnp.dot(kt, dsbuf[...], preferred_element_type=jnp.float32) * scale
                for i in range(group):
                    dqbuf[h, sub, layer, :, i * HD : (i + 1) * HD] = jnp.transpose(
                        dqt[:, i * rows : (i + 1) * rows]
                    ).astype(jnp.bfloat16)
            return unused

        lax.fori_loop(0, 2, sub_step, 0)

        for slot in range(blocks):
            at = slice(slot * rows, (slot + 1) * rows)
            sbuf[h, slot, 0] = (acc[0, at] * scale).astype(jnp.bfloat16)
            sbuf[h, slot, 1] = acc[1, at].astype(jnp.bfloat16)
        own = pl.ds(pl.multiple_of(sec * piece, piece), piece)
        rbuf[0, sec, core, h] = sbuf[h, reach + core, :, own]
        for slot in range(blocks):
            for t in range(sections):
                if slot < reach:
                    condition = 2 * chip - reach + slot >= 0
                elif t == 0:
                    condition = core != slot - reach
                else:
                    condition = None
                if condition is None:
                    g_copy(h, slot, t).start()
                else:
                    pl.when(condition)(lambda: g_copy(h, slot, t).start())
        dq_copy(h).start()
        dq_local(h).start()
        return unused

    lax.fori_loop(0, heads, head_step, 0)

    for h in range(heads):
        for d in range(depth + 1):
            for s in range(sections):
                for c in range(2):
                    if d == 0:
                        condition = (sec != s) | (core != c)
                    else:
                        condition = chip + d < chips

                    @pl.when(condition)
                    def _():
                        g_wait(h, d, s, c).wait_recv()
    for c in range(2):
        for h in range(heads):
            total = None
            for d in range(depth + 1):
                for s in range(sections):
                    term = rbuf[d, s, c, h].astype(jnp.float32)
                    total = term if total is None else total + term
            g = c * heads + h
            out_ref[:, :, g * HD : (g + 1) * HD] = total.astype(jnp.bfloat16)

    def finish(h, unused):
        dq_wait(h).wait_recv()
        dq_copy(h).wait_send()
        dq_local(h).wait()
        for copy in q_copies(h):
            copy.wait_send()
        kv_copy(h, 0, 1).wait_send()
        for d in range(1, depth + 1):
            @pl.when(chip + d < chips)
            def _():
                for w in range(2):
                    kv_copy(h, d, w).wait_send()
        for slot in range(blocks):
            for t in range(sections):
                if slot < reach:
                    condition = 2 * chip - reach + slot >= 0
                elif t == 0:
                    condition = core != slot - reach
                else:
                    condition = None
                if condition is None:
                    g_copy(h, slot, t).wait_send()
                else:
                    pl.when(condition)(lambda: g_copy(h, slot, t).wait_send())
        return unused

    lax.fori_loop(0, heads, finish, 0)


def body(queries, grad_out, keys_values, doc_ids):
    layers, rows, width = queries.shape
    kv_width = keys_values.shape[2]
    heads_kv = kv_width // HD
    group = width // kv_width
    n = lax.axis_size("ctx")
    sections = lax.axis_size("section")
    reach = n // 4
    heads = heads_kv // 2
    blocks = reach + 2
    window = (reach + 1) * rows
    piece = rows // sections
    depth = reach // 2
    bf, f32 = jnp.bfloat16, jnp.float32
    dma = pltpu.SemaphoreType.DMA
    hbm = pl.BlockSpec(memory_space=pl.ANY)
    vmem = pl.BlockSpec(memory_space=pltpu.VMEM)
    return pl.pallas_call(
        functools.partial(kernel, n, sections, reach, heads_kv, group),
        out_shape=(
            jax.ShapeDtypeStruct(queries.shape, bf),
            jax.ShapeDtypeStruct((2, piece, kv_width), bf),
        ),
        in_specs=[hbm, hbm, hbm, vmem],
        out_specs=(hbm, vmem),
        scratch_shapes=[
            pltpu.VMEM((heads, 2, layers, rows, group * HD), bf),
            pltpu.VMEM((heads, 2, layers, rows, group * HD), bf),
            pltpu.VMEM((heads, 2, blocks, rows, HD), bf),
            pltpu.VMEM((2, window, rows), f32),
            pltpu.VMEM((window, group * rows), bf),
            pltpu.VMEM((window, group * rows), bf),
            pltpu.VMEM((2, blocks * rows, HD), f32),
            pltpu.VMEM((heads, blocks, 2, rows, HD), bf),
            pltpu.VMEM((depth + 1, sections, 2, heads, 2, piece, HD), bf),
            pltpu.VMEM((heads, 2, layers, rows, group * HD), bf),
            dma((heads, 3)),
            dma((heads, 2)),
            dma((heads, 2)),
            dma((heads, depth + 1, 2)),
            dma((heads, blocks)),
            dma((heads, blocks, sections)),
            dma((depth + 1, sections, 2, heads)),
            dma((heads,)),
            dma((heads,)),
            dma((heads,)),
        ],
        compiler_params=pltpu.CompilerParams(
            collective_id=0, has_side_effects=True, vmem_limit_bytes=48 * 1024 * 1024
        ),
        name="cross_backward",
    )(queries, grad_out, keys_values, doc_ids.reshape(-1, rows))


def solution(mesh):
    return jax.shard_map(
        body,
        mesh=mesh,
        in_specs=(P("section", "ctx", None), P("section", "ctx", None), P(None, "ctx", None), P()),
        out_specs=(P("section", "ctx", None), P(None, ("ctx", "section"), None)),
        check_vma=False,
    )
```

time: 162 us -> 36.9 us (0.23)
  waiting for transfers between devices: 40.6 us -> 0 us
  matrix products: 30.7 us -> 0 us
  Pallas kernels: 0 us -> 30.6 us
  local copies, waits for them, and re-layouts: 29.5 us -> 5.31 us
  starting transfers between devices: 20.9 us -> 0 us
  between operations: 14.3 us -> 0.65 us
  loops' own time: 13.1 us -> 0 us
  other arithmetic: 12.1 us -> 0 us
    dot_general x28 -> x0, matrix products: 30.7 us -> none  [the longest x8 11 us: block_scores(): jnp.einsum('ltgnd,kgd->ltgnk', qrows, kpart, preferred_element_type=jnp.f...]
    pallas_call x0 -> x1, Pallas kernels: none -> 30.6 us  [body(): pl.pallas_call(functools.partial(kernel, n, sections, reach, heads_kv, gr...]
    ppermute x8 -> x0, waiting for transfers between devices: 21.3 us -> none  [from_behind(): lax.ppermute(value, axis, [(source, source + steps) for source in range(f...]
    ppermute x8 -> x0, starting transfers between devices: 20.8 us -> none  [from_behind(): lax.ppermute(value, axis, [(source, source + steps) for source in range(f...]
    reduce_scatter x1 -> x0, waiting for transfers between devices: 19.3 us -> none  [body(): lax.psum_scatter(collected.astype(jnp.bfloat16), 'section', scatter_dimen...]
    another operation x12 -> x0, loops' own time: 13.1 us -> none  [the longest x1 6.39 us: body(): lax.scan(backward_step, jnp.zeros(stat_shape + (HD,), jnp.float32), jnp.a...]
    dynamic_slice x31 -> x0, local copies, waits for them, and re-layouts: 8.24 us -> none  [the longest x10 5.98 us: body(): lax.scan(forward_step, start_state, jnp.arange(nblocks, dtype=jnp.int32))]
    reduce_or x10 -> x0, other arithmetic: 7.74 us -> none  [the longest x5 4.06 us: backward_step(): return lax.cond(jnp.any(visible), backward_compute, skipped, dquery)]
  transfers between devices with their start and end apart: 9 -> 0, of which waited for: 5 -> 0; matrix products, arithmetic and copies ran while one was open for 5% -> 0% of each run, Pallas kernels for 0% -> 0%
where the time goes in v1:
time: 36.9 us; the launch traced here: 36.6 us
  Pallas kernels  30.6 us (83%)
  local copies, waits for them, and re-layouts  5.31 us (14%)
  between operations  0.65 us (2%)
    pallas_call x1, Pallas kernels, body(): pl.pallas_call(functools.partial(kernel, n, sections, reach, heads_kv, gr...  30.6 us
    unnamed x10, local copies, waits for them, and re-layouts  5.31 us

profile of v1, /device:TPU:13, one launch (start us, length us, event | category | flops | bytes accessed | tf_op | source)
XLA Modules:
  0.0 36.6 jit_solution(12583219845487213739)
XLA Ops:
  0.6 0.0 copy-start
  0.6 1.1 %copy-done = bf16[1,128,2560]{2,1,0:T(8,128)(2,1)S(1)} copy-done((bf16[1,128,2560]{2,1,0:T(8,128)(2,1)S(1)}, bf16[1,128,2560]{2,1,0:T(8,128)(2,1)}, u32[]{:S(2)}) %copy-start) | copy-done | bytes 655384
  1.7 0.0 copy-start.1
  1.7 1.1 %copy-done.1 = bf16[1,128,2560]{2,1,0:T(8,128)(2,1)S(1)} copy-done((bf16[1,128,2560]{2,1,0:T(8,128)(2,1)S(1)}, bf16[1,128,2560]{2,1,0:T(8,128)(2,1)}, u32[]{:S(2)}) %copy-start.1) | copy-done | bytes 655384
  2.8 0.0 copy-start.2
  2.8 0.9 %copy-done.2 = bf16[2,128,512]{2,1,0:T(8,128)(2,1)S(1)} copy-done((bf16[2,128,512]{2,1,0:T(8,128)(2,1)S(1)}, bf16[2,128,512]{2,1,0:T(8,128)(2,1)}, u32[]{:S(2)}) %copy-start.2) | copy-done | bytes 262168
  3.8 0.0 copy-start.3
  3.8 0.7 %copy-done.3 = s32[2048]{0:T(1024)S(1)} copy-done((s32[2048]{0:T(1024)S(1)}, s32[2048]{0:T(1024)}, u32[]{:S(2)}) %copy-start.3) | copy-done | bytes 8216
  4.5 30.6 %cross_backward.1 = (bf16[1,128,2560]{2,1,0:T(8,128)(2,1)S(1)}, bf16[2,64,512]{2,1,0:T(8,128)(2,1)S(1)}) custom-call(bf16[1,128,2560]{2,1,0:T(8,128)(2,1)S(1)} %copy-done, bf16[1,128,2560]{2,1,0:T(8,128)(2,1)S(1)} %copy-done.1, bf16[2,128,512]{2,1,0:T(8,128)(2,1)S(1)} %copy-done.2, s32[16,128]{1,0:T(8,128)S(1)} %bitcast.1), custom_call_target="tpu_custom_call" | custom-call | tf_op jit(solution)/shard_map/cross_backward/pallas_call | solution.py:334
  35.1 0.8 %copy.8 = bf16[1,128,2560]{2,1,0:T(8,128)(2,1)} copy(bf16[1,128,2560]{2,1,0:T(8,128)(2,1)S(1)} %get-tuple-element.4) | data formatting | bytes 1310720
  36.0 0.7 %copy.9 = bf16[2,64,512]{2,1,0:T(8,128)(2,1)} copy(bf16[2,64,512]{2,1,0:T(8,128)(2,1)S(1)} %get-tuple-element.5) | data formatting | bytes 262144
Async XLA Ops:
  0.6 1.1 %copy-start = (bf16[1,128,2560]{2,1,0:T(8,128)(2,1)S(1)}, bf16[1,128,2560]{2,1,0:T(8,128)(2,1)}, u32[]{:S(2)}) copy-start(bf16[1,128,2560]{2,1,0:T(8,128)(2,1)} %q_ref.1) | copy-start | bytes 1966084
  1.7 1.1 %copy-start.1 = (bf16[1,128,2560]{2,1,0:T(8,128)(2,1)S(1)}, bf16[1,128,2560]{2,1,0:T(8,128)(2,1)}, u32[]{:S(2)}) copy-start(bf16[1,128,2560]{2,1,0:T(8,128)(2,1)} %do_ref.1) | copy-start | bytes 1966084
  2.8 0.9 %copy-start.2 = (bf16[2,128,512]{2,1,0:T(8,128)(2,1)S(1)}, bf16[2,128,512]{2,1,0:T(8,128)(2,1)}, u32[]{:S(2)}) copy-start(bf16[2,128,512]{2,1,0:T(8,128)(2,1)} %kv_ref.1) | copy-start | bytes 786436
  3.8 0.7 %copy-start.3 = (s32[2048]{0:T(1024)S(1)}, s32[2048]{0:T(1024)}, u32[]{:S(2)}) copy-start(s32[2048]{0:T(1024)} %param.7) | copy-start | bytes 24580

commit v2 on v1

--- a/solution.py
+++ b/solution.py
@@ -17,17 +17,19 @@
     n, sections, reach, heads_kv, group,
     q_ref, do_ref, kv_ref, docs_ref,
     dq_ref, out_ref,
-    qbuf, dobuf, kvbuf, bias, pbuf, dsbuf, acc, sbuf, rbuf, dqbuf,
-    lsem, qsend, qrecv, kvsend, kvrecv, gsend, grecv, dqsend, dqrecv, dqloc,
+    docs, qbuf, dobuf, kvbuf, bias, pbuf, dsbuf, acc, sbuf, rbuf, dqbuf,
+    docsem, lsem, qsend, qrecv, kvsend, kvrecv, relsend, gsend, grecv, dqsend, dqrecv, dqloc,
 ):
     me = lax.axis_index("ctx")
     sec = lax.axis_index("section")
-    layers, rows = q_ref.shape[0], q_ref.shape[1]
+    rows = kv_ref.shape[1]
+    layers = q_ref.shape[0] // rows
     core = lax.rem(me, 2)
     other = 1 - core
     chip = me // 2
     chips = n // 2
     depth = reach // 2
+    place = lax.rem(chip, depth)
     blocks = reach + 2
     heads = heads_kv // 2
     gw = group * HD
@@ -44,8 +46,8 @@
     def local_copies(h):
         g = core * heads + h
         return [
-            pltpu.make_async_copy(q_ref.at[:, :, cols(g, gw)], qbuf.at[h, core], lsem.at[h, 0]),
-            pltpu.make_async_copy(do_ref.at[:, :, cols(g, gw)], dobuf.at[h, core], lsem.at[h, 1]),
+            pltpu.make_async_copy(q_ref.at[:, cols(g, gw)], qbuf.at[h, core], lsem.at[h, 0]),
+            pltpu.make_async_copy(do_ref.at[:, cols(g, gw)], dobuf.at[h, core], lsem.at[h, 1]),
             pltpu.make_async_copy(
                 kv_ref.at[:, :, cols(g, HD)], kvbuf.at[h, :, reach + core], lsem.at[h, 2]
             ),
@@ -56,7 +58,7 @@
         partner = dev(2 * chip + other, sec)
         return [
             pltpu.make_async_remote_copy(
-                src_ref=src.at[:, :, cols(g, gw)], dst_ref=dst.at[h, core],
+                src_ref=src.at[:, cols(g, gw)], dst_ref=dst.at[h, core],
                 send_sem=qsend.at[h, k], recv_sem=qrecv.at[h, k],
                 device_id=partner, device_id_type=MESH,
             )
@@ -79,6 +81,28 @@
             device_id=dev(2 * chip + other, sec), device_id_type=MESH,
         )
 
+    def relay_copy(h, step, w):
+        slot = 2 * step + w
+        return pltpu.make_async_remote_copy(
+            src_ref=kvbuf.at[h, :, w], dst_ref=kvbuf.at[h, :, slot],
+            send_sem=relsend.at[h, step - 1, w], recv_sem=kvrecv.at[h, slot],
+            device_id=dev(2 * (chip - step) + core, sec), device_id_type=MESH,
+        )
+
+    def direct(d):
+        return (chip + d < chips) & (place + d < depth) if d < depth else chip + d < chips
+
+    def relays(step):
+        return (place >= step) & (chip >= depth)
+
+    def relay(h):
+        for w in range(2):
+            @pl.when(chip >= depth)
+            def _():
+                kv_wait(h, w).wait_recv()
+            for step in range(1, depth):
+                pl.when(relays(step))(lambda: relay_copy(h, step, w).start())
+
     def g_copy(h, slot, t):
         d = (reach + 1 - slot) // 2
         owner_core = (slot - reach) % 2
@@ -99,21 +123,21 @@
 
     def dq_copy(h):
         return pltpu.make_async_remote_copy(
-            src_ref=dqbuf.at[h, other], dst_ref=dq_ref.at[:, :, cols(core * heads + h, gw)],
+            src_ref=dqbuf.at[h, other], dst_ref=dq_ref.at[:, cols(core * heads + h, gw)],
             send_sem=dqsend.at[h], recv_sem=dqrecv.at[h],
             device_id=dev(2 * chip + other, sec), device_id_type=MESH,
         )
 
     def dq_wait(h):
         return pltpu.make_async_remote_copy(
-            src_ref=dqbuf.at[h, other], dst_ref=dq_ref.at[:, :, cols(other * heads + h, gw)],
+            src_ref=dqbuf.at[h, other], dst_ref=dq_ref.at[:, cols(other * heads + h, gw)],
             send_sem=dqsend.at[h], recv_sem=dqrecv.at[h],
             device_id=dev(2 * chip + other, sec), device_id_type=MESH,
         )
 
     def dq_local(h):
         return pltpu.make_async_copy(
-            dqbuf.at[h, core], dq_ref.at[:, :, cols(core * heads + h, gw)], dqloc.at[h]
+            dqbuf.at[h, core], dq_ref.at[:, cols(core * heads + h, gw)], dqloc.at[h]
         )
 
     barrier = pltpu.get_barrier_semaphore()
@@ -130,6 +154,8 @@
                         device_id_type=MESH,
                     )
 
+    docs_copy = pltpu.make_async_copy(docs_ref, docs, docsem)
+    docs_copy.start()
     for h in range(heads):
         for copy in local_copies(h):
             copy.start()
@@ -139,7 +165,7 @@
 
     for h in range(heads):
         for d in range(depth, 0, -1):
-            @pl.when(chip + d < chips)
+            @pl.when(direct(d))
             def _():
                 for w in range(2):
                     kv_copy(h, d, w).start()
@@ -158,24 +184,60 @@
         def _():
             rbuf[d] = jnp.zeros(rbuf.shape[1:], jnp.bfloat16)
 
+    docs_copy.wait()
     row_at = lax.broadcasted_iota(jnp.int32, (rows, rows), 0)
     col_at = lax.broadcasted_iota(jnp.int32, (rows, rows), 1)
     for slot in range(blocks):
         at = 2 * chip - reach + slot
-        kdoc = docs_ref[pl.ds(jnp.maximum(at, 0), 1), :].astype(jnp.float32)
+        kdoc = docs[pl.ds(jnp.maximum(at, 0), 1), :].astype(jnp.float32)
         kdoc = jnp.transpose(jnp.broadcast_to(kdoc, (rows, rows)))
         for sub in range(2):
             if not 0 <= slot - sub <= reach:
                 continue
-            qdoc = docs_ref[pl.ds(2 * chip + sub, 1), :].astype(jnp.float32)
+            qdoc = docs[pl.ds(2 * chip + sub, 1), :].astype(jnp.float32)
             kplace = at * rows + row_at
             qplace = (2 * chip + sub) * rows + col_at
             seen = (kplace <= qplace) & (kplace >= 0) & (kdoc == qdoc)
             bias[sub, (slot - sub) * rows : (slot - sub + 1) * rows] = jnp.where(seen, 0.0, NEG)
 
+    def score_part(h, sub):
+        k = kvbuf[h, 0, pl.ds(sub, reach + 1)].reshape(window, HD)
+        v = kvbuf[h, 1, pl.ds(sub, reach + 1)].reshape(window, HD)
+        nt = (((1,), (1,)), ((), ()))
+        for i in range(group):
+            at = slice(i * HD, (i + 1) * HD)
+            s = lax.dot_general(k, qbuf[h, sub, :, at], nt, preferred_element_type=jnp.float32)
+            dp = lax.dot_general(v, dobuf[h, sub, :, at], nt, preferred_element_type=jnp.float32)
+            s = s * (scale * LOG2E) + jnp.concatenate([bias[sub]] * layers, axis=1)
+            e = jnp.exp2(s - jnp.max(s, axis=0, keepdims=True))
+            inverse = 1.0 / jnp.sum(e, axis=0, keepdims=True)
+            delta = jnp.sum(e * dp, axis=0, keepdims=True) * inverse
+            p = (e * inverse).astype(jnp.bfloat16)
+            to = slice(i * layers * rows, (i + 1) * layers * rows)
+            pbuf[:, to] = p
+            dsbuf[:, to] = (p.astype(jnp.float32) * (dp - delta)).astype(jnp.bfloat16)
+
+    def key_part(h, sub):
+        keys_at = pl.ds(pl.multiple_of(sub * rows, rows), window)
+        for k, (weights, buf) in enumerate([(dsbuf, qbuf), (pbuf, dobuf)]):
+            stack = jnp.concatenate(
+                [buf[h, sub, :, i * HD : (i + 1) * HD] for i in range(group)], axis=0
+            )
+            acc[k, keys_at] += jnp.dot(weights[...], stack, preferred_element_type=jnp.float32)
+
+    def query_part(h, sub):
+        kt = jnp.transpose(kvbuf[h, 0, pl.ds(sub, reach + 1)].reshape(window, HD))
+        dqt = jnp.dot(kt, dsbuf[...], preferred_element_type=jnp.float32) * scale
+        for i in range(group):
+            dqbuf[h, sub, :, i * HD : (i + 1) * HD] = jnp.transpose(
+                dqt[:, i * layers * rows : (i + 1) * layers * rows]
+            ).astype(jnp.bfloat16)
+
+    relay(0)
+
     def head_step(h, unused):
         local_copies(h)[2].wait()
-        for slot in range(blocks):
+        for slot in range(2, blocks):
             at = 2 * chip - reach + slot
             if slot < reach:
                 condition = at >= 0
@@ -187,58 +249,21 @@
                 kv_wait(h, slot).wait_recv()
 
         acc[...] = jnp.zeros_like(acc)
-
-        def sub_step(w, unused):
-            sub = lax.rem(core + w, 2)
-
-            @pl.when(w == 0)
-            def _():
-                for copy in local_copies(h)[:2]:
-                    copy.wait()
-
-            @pl.when(w == 1)
-            def _():
-                for copy in q_copies(h):
-                    copy.wait_recv()
-
-            k = kvbuf[h, 0, pl.ds(sub, reach + 1)].reshape(window, HD)
-            v = kvbuf[h, 1, pl.ds(sub, reach + 1)].reshape(window, HD)
-            kt = jnp.transpose(k)
-            keys_at = pl.ds(pl.multiple_of(sub * rows, rows), window)
-            for layer in range(layers):
-                for i in range(group):
-                    at = pl.ds(i * HD, HD)
-                    q = qbuf[h, sub, layer, :, at]
-                    do = dobuf[h, sub, layer, :, at]
-                    nt = (((1,), (1,)), ((), ()))
-                    s = lax.dot_general(k, q, nt, preferred_element_type=jnp.float32)
-                    dp = lax.dot_general(v, do, nt, preferred_element_type=jnp.float32)
-                    s = s * (scale * LOG2E) + bias[sub]
-                    e = jnp.exp2(s - jnp.max(s, axis=0, keepdims=True))
-                    inverse = 1.0 / jnp.sum(e, axis=0, keepdims=True)
-                    delta = jnp.sum(e * dp, axis=0, keepdims=True) * inverse
-                    p = (e * inverse).astype(jnp.bfloat16)
-                    pbuf[:, i * rows : (i + 1) * rows] = p
-                    dsbuf[:, i * rows : (i + 1) * rows] = (
-                        p.astype(jnp.float32) * (dp - delta)
-                    ).astype(jnp.bfloat16)
-                stack_q = jnp.concatenate(
-                    [qbuf[h, sub, layer, :, i * HD : (i + 1) * HD] for i in range(group)], axis=0
-                )
-                stack_do = jnp.concatenate(
-                    [dobuf[h, sub, layer, :, i * HD : (i + 1) * HD] for i in range(group)], axis=0
-                )
-                acc[0, keys_at] += jnp.dot(dsbuf[...], stack_q, preferred_element_type=jnp.float32)
-                acc[1, keys_at] += jnp.dot(pbuf[...], stack_do, preferred_element_type=jnp.float32)
-                dqt = jnp.dot(kt, dsbuf[...], preferred_element_type=jnp.float32) * scale
-                for i in range(group):
-                    dqbuf[h, sub, layer, :, i * HD : (i + 1) * HD] = jnp.transpose(
-                        dqt[:, i * rows : (i + 1) * rows]
-                    ).astype(jnp.bfloat16)
-            return unused
-
-        lax.fori_loop(0, 2, sub_step, 0)
-
+        for copy in local_copies(h)[:2]:
+            copy.wait()
+        score_part(h, core)
+        key_part(h, core)
+        query_part(h, core)
+        dq_local(h).start()
+
+        @pl.when(h + 1 < heads)
+        def _():
+            relay(h + 1)
+
+        for copy in q_copies(h):
+            copy.wait_recv()
+        score_part(h, other)
+        key_part(h, other)
         for slot in range(blocks):
             at = slice(slot * rows, (slot + 1) * rows)
             sbuf[h, slot, 0] = (acc[0, at] * scale).astype(jnp.bfloat16)
@@ -257,8 +282,8 @@
                     g_copy(h, slot, t).start()
                 else:
                     pl.when(condition)(lambda: g_copy(h, slot, t).start())
+        query_part(h, other)
         dq_copy(h).start()
-        dq_local(h).start()
         return unused
 
     lax.fori_loop(0, heads, head_step, 0)
@@ -293,10 +318,13 @@
             copy.wait_send()
         kv_copy(h, 0, 1).wait_send()
         for d in range(1, depth + 1):
-            @pl.when(chip + d < chips)
+            @pl.when(direct(d))
             def _():
                 for w in range(2):
                     kv_copy(h, d, w).wait_send()
+        for step in range(1, depth):
+            for w in range(2):
+                pl.when(relays(step))(lambda: relay_copy(h, step, w).wait_send())
         for slot in range(blocks):
             for t in range(sections):
                 if slot < reach:
@@ -331,30 +359,33 @@
     dma = pltpu.SemaphoreType.DMA
     hbm = pl.BlockSpec(memory_space=pl.ANY)
     vmem = pl.BlockSpec(memory_space=pltpu.VMEM)
-    return pl.pallas_call(
+    grad_queries, grad_kv = pl.pallas_call(
         functools.partial(kernel, n, sections, reach, heads_kv, group),
         out_shape=(
-            jax.ShapeDtypeStruct(queries.shape, bf),
+            jax.ShapeDtypeStruct((layers * rows, width), bf),
             jax.ShapeDtypeStruct((2, piece, kv_width), bf),
         ),
-        in_specs=[hbm, hbm, hbm, vmem],
+        in_specs=[hbm, hbm, hbm, hbm],
         out_specs=(hbm, vmem),
         scratch_shapes=[
-            pltpu.VMEM((heads, 2, layers, rows, group * HD), bf),
-            pltpu.VMEM((heads, 2, layers, rows, group * HD), bf),
+            pltpu.VMEM((n, rows), jnp.int32),
+            pltpu.VMEM((heads, 2, layers * rows, group * HD), bf),
+            pltpu.VMEM((heads, 2, layers * rows, group * HD), bf),
             pltpu.VMEM((heads, 2, blocks, rows, HD), bf),
             pltpu.VMEM((2, window, rows), f32),
-            pltpu.VMEM((window, group * rows), bf),
-            pltpu.VMEM((window, group * rows), bf),
+            pltpu.VMEM((window, group * layers * rows), bf),
+            pltpu.VMEM((window, group * layers * rows), bf),
             pltpu.VMEM((2, blocks * rows, HD), f32),
             pltpu.VMEM((heads, blocks, 2, rows, HD), bf),
             pltpu.VMEM((depth + 1, sections, 2, heads, 2, piece, HD), bf),
-            pltpu.VMEM((heads, 2, layers, rows, group * HD), bf),
+            pltpu.VMEM((heads, 2, layers * rows, group * HD), bf),
+            dma,
             dma((heads, 3)),
             dma((heads, 2)),
             dma((heads, 2)),
             dma((heads, depth + 1, 2)),
             dma((heads, blocks)),
+            dma((heads, max(depth - 1, 1), 2)),
             dma((heads, blocks, sections)),
             dma((depth + 1, sections, 2, heads)),
             dma((heads,)),
@@ -362,10 +393,14 @@
             dma((heads,)),
         ],
         compiler_params=pltpu.CompilerParams(
-            collective_id=0, has_side_effects=True, vmem_limit_bytes=48 * 1024 * 1024
+            collective_id=0, has_side_effects=True, vmem_limit_bytes=67043328
         ),
         name="cross_backward",
-    )(queries, grad_out, keys_values, doc_ids.reshape(-1, rows))
+    )(
+        queries.reshape(layers * rows, width), grad_out.reshape(layers * rows, width),
+        keys_values, doc_ids.reshape(n, rows),
+    )
+    return grad_queries.reshape(queries.shape), grad_kv
 
 
 def solution(mesh):

time: 36.9 us -> 34.9 us (0.946)
  local copies, waits for them, and re-layouts: 5.31 us -> 2.66 us
  Pallas kernels: 30.6 us -> 31.4 us
    unnamed x10 -> x4, local copies, waits for them, and re-layouts: 5.31 us -> 2.66 us
    pallas_call x1, Pallas kernels: 30.6 us -> 31.4 us  [body(): pl.pallas_call(functools.partial(kernel, n, sections, reach, heads_kv, gr...]
where the time goes in v2:
time: 34.9 us; the launch traced here: 34.7 us
  Pallas kernels  31.4 us (90%)
  local copies, waits for them, and re-layouts  2.66 us (8%)
  between operations  0.65 us (2%)
    pallas_call x1, Pallas kernels, body(): pl.pallas_call(functools.partial(kernel, n, sections, reach, heads_kv, gr...  31.4 us
    unnamed x4, local copies, waits for them, and re-layouts  2.66 us

profile of v2, /device:TPU:13, one launch (start us, length us, event | category | flops | bytes accessed | tf_op | source)
XLA Modules:
  0.0 34.7 jit_solution(4509667948300752321)
XLA Ops:
  0.6 31.4 %cross_backward.1 = (bf16[128,2560]{1,0:T(8,128)(2,1)}, bf16[2,64,512]{2,1,0:T(8,128)(2,1)}) custom-call(bf16[128,2560]{1,0:T(8,128)(2,1)} %bitcast.4, bf16[128,2560]{1,0:T(8,128)(2,1)} %bitcast.5, bf16[2,128,512]{2,1,0:T(8,128)(2,1)} %kv_ref.1, s32[16,128]{1,0:T(8,128)} %bitcast.7), custom_call_target="tpu_custom_call" | custom-call | tf_op jit(solution)/shard_map/cross_backward/pallas_call | solution.py:362
  32.1 0.0 copy-start
  32.1 2.0 %copy.8 = bf16[1,128,2560]{2,1,0:T(8,128)(2,1)} copy(bf16[1,128,2560]{2,1,0:T(8,128)(2,1)} %bitcast.6) | data formatting | bytes 1310720
  34.1 0.0 copy-done
  34.1 0.7 %copy.9 = bf16[2,64,512]{2,1,0:T(8,128)(2,1)} copy(bf16[2,64,512]{2,1,0:T(8,128)(2,1)S(1)} %copy-done) | data formatting | bytes 262144
Async XLA Ops:
  32.1 2.0 %copy-start = (bf16[2,64,512]{2,1,0:T(8,128)(2,1)S(1)}, bf16[2,64,512]{2,1,0:T(8,128)(2,1)}, u32[]{:S(2)}) copy-start(bf16[2,64,512]{2,1,0:T(8,128)(2,1)} %get-tuple-element.9) | copy-start | bytes 393220

commit v3 on v2

--- a/solution.py
+++ b/solution.py
@@ -141,18 +141,26 @@
         )
 
     barrier = pltpu.get_barrier_semaphore()
+
+    def greet(ctx, section):
+        pl.semaphore_signal(barrier, inc=1, device_id=dev(ctx, section), device_id_type=MESH)
+
     for step in range(-depth, depth + 1):
-        @pl.when((chip + step >= 0) & (chip + step < chips))
+        if abs(step) == depth:
+            condition = (chip + step >= 0) & (chip + step < chips)
+        else:
+            condition = (place + step >= 0) & (place + step < depth)
+
+        @pl.when(condition)
         def _():
             for w in range(2):
-                for t in range(sections):
-                    if step == 0 and w == 0 and t == 0:
-                        continue
-                    pl.semaphore_signal(
-                        barrier, inc=1,
-                        device_id=dev(2 * (chip + step) + lax.rem(core + w, 2), lax.rem(sec + t, sections)),
-                        device_id_type=MESH,
-                    )
+                if step == 0 and w == 0:
+                    continue
+                greet(2 * (chip + step) + lax.rem(core + w, 2), sec)
+
+    for w in range(2):
+        for t in range(1, sections):
+            greet(2 * chip + lax.rem(core + w, 2), lax.rem(sec + t, sections))
 
     docs_copy = pltpu.make_async_copy(docs_ref, docs, docsem)
     docs_copy.start()
@@ -160,8 +168,8 @@
         for copy in local_copies(h):
             copy.start()
 
-    near = jnp.minimum(chip, depth) + jnp.minimum(chips - 1 - chip, depth) + 1
-    pl.semaphore_wait(barrier, near * (2 * sections) - 1)
+    near = depth + (chip >= depth).astype(jnp.int32) + (chip + depth < chips).astype(jnp.int32)
+    pl.semaphore_wait(barrier, 2 * near - 1 + 2 * (sections - 1))
 
     for h in range(heads):
         for d in range(depth, 0, -1):
@@ -215,11 +223,11 @@
             p = (e * inverse).astype(jnp.bfloat16)
             to = slice(i * layers * rows, (i + 1) * layers * rows)
             pbuf[:, to] = p
-            dsbuf[:, to] = (p.astype(jnp.float32) * (dp - delta)).astype(jnp.bfloat16)
+            dsbuf[h, sub, :, to] = (p.astype(jnp.float32) * (dp - delta)).astype(jnp.bfloat16)
 
     def key_part(h, sub):
         keys_at = pl.ds(pl.multiple_of(sub * rows, rows), window)
-        for k, (weights, buf) in enumerate([(dsbuf, qbuf), (pbuf, dobuf)]):
+        for k, (weights, buf) in enumerate([(dsbuf.at[h, sub], qbuf), (pbuf, dobuf)]):
             stack = jnp.concatenate(
                 [buf[h, sub, :, i * HD : (i + 1) * HD] for i in range(group)], axis=0
             )
@@ -227,7 +235,7 @@
 
     def query_part(h, sub):
         kt = jnp.transpose(kvbuf[h, 0, pl.ds(sub, reach + 1)].reshape(window, HD))
-        dqt = jnp.dot(kt, dsbuf[...], preferred_element_type=jnp.float32) * scale
+        dqt = jnp.dot(kt, dsbuf[h, sub], preferred_element_type=jnp.float32) * scale
         for i in range(group):
             dqbuf[h, sub, :, i * HD : (i + 1) * HD] = jnp.transpose(
                 dqt[:, i * layers * rows : (i + 1) * layers * rows]
@@ -253,8 +261,6 @@
             copy.wait()
         score_part(h, core)
         key_part(h, core)
-        query_part(h, core)
-        dq_local(h).start()
 
         @pl.when(h + 1 < heads)
         def _():
@@ -282,11 +288,18 @@
                     g_copy(h, slot, t).start()
                 else:
                     pl.when(condition)(lambda: g_copy(h, slot, t).start())
+        return unused
+
+    lax.fori_loop(0, heads, head_step, 0)
+
+    def query_step(h, unused):
         query_part(h, other)
         dq_copy(h).start()
+        query_part(h, core)
+        dq_local(h).start()
         return unused
 
-    lax.fori_loop(0, heads, head_step, 0)
+    lax.fori_loop(0, heads, query_step, 0)
 
     for h in range(heads):
         for d in range(depth + 1):
@@ -374,7 +387,7 @@
             pltpu.VMEM((heads, 2, blocks, rows, HD), bf),
             pltpu.VMEM((2, window, rows), f32),
             pltpu.VMEM((window, group * layers * rows), bf),
-            pltpu.VMEM((window, group * layers * rows), bf),
+            pltpu.VMEM((heads, 2, window, group * layers * rows), bf),
             pltpu.VMEM((2, blocks * rows, HD), f32),
             pltpu.VMEM((heads, blocks, 2, rows, HD), bf),
             pltpu.VMEM((depth + 1, sections, 2, heads, 2, piece, HD), bf),

time: 34.9 us -> 34.7 us (level)
  no operation moved by 1% of the time
where the time goes in v3:
time: 34.7 us; the launch traced here: 34.5 us
  Pallas kernels  31.2 us (90%)
  local copies, waits for them, and re-layouts  2.66 us (8%)
  between operations  0.65 us (2%)
    pallas_call x1, Pallas kernels, body(): pl.pallas_call(functools.partial(kernel, n, sections, reach, heads_kv, gr...  31.2 us
    unnamed x4, local copies, waits for them, and re-layouts  2.66 us

profile of v3, /device:TPU:13, one launch (start us, length us, event | category | flops | bytes accessed | tf_op | source)
XLA Modules:
  0.0 34.5 jit_solution(12853268042117253396)
XLA Ops:
  0.6 31.2 %cross_backward.1 = (bf16[128,2560]{1,0:T(8,128)(2,1)}, bf16[2,64,512]{2,1,0:T(8,128)(2,1)}) custom-call(bf16[128,2560]{1,0:T(8,128)(2,1)} %bitcast.4, bf16[128,2560]{1,0:T(8,128)(2,1)} %bitcast.5, bf16[2,128,512]{2,1,0:T(8,128)(2,1)} %kv_ref.1, s32[16,128]{1,0:T(8,128)} %bitcast.7), custom_call_target="tpu_custom_call" | custom-call | tf_op jit(solution)/shard_map/cross_backward/pallas_call | solution.py:375
  31.9 0.0 copy-start
  31.9 2.0 %copy.8 = bf16[1,128,2560]{2,1,0:T(8,128)(2,1)} copy(bf16[1,128,2560]{2,1,0:T(8,128)(2,1)} %bitcast.6) | data formatting | bytes 1310720
  33.9 0.0 copy-done
  33.9 0.7 %copy.9 = bf16[2,64,512]{2,1,0:T(8,128)(2,1)} copy(bf16[2,64,512]{2,1,0:T(8,128)(2,1)S(1)} %copy-done) | data formatting | bytes 262144
Async XLA Ops:
  31.9 2.0 %copy-start = (bf16[2,64,512]{2,1,0:T(8,128)(2,1)S(1)}, bf16[2,64,512]{2,1,0:T(8,128)(2,1)}, u32[]{:S(2)}) copy-start(bf16[2,64,512]{2,1,0:T(8,128)(2,1)} %get-tuple-element.9) | copy-start | bytes 393220

commit v4 on v3

--- a/solution.py
+++ b/solution.py
@@ -17,8 +17,8 @@
     n, sections, reach, heads_kv, group,
     q_ref, do_ref, kv_ref, docs_ref,
     dq_ref, out_ref,
-    docs, qbuf, dobuf, kvbuf, bias, pbuf, dsbuf, acc, sbuf, rbuf, dqbuf,
-    docsem, lsem, qsend, qrecv, kvsend, kvrecv, relsend, gsend, grecv, dqsend, dqrecv, dqloc,
+    docs, qbuf, dobuf, kvbuf, bias, pbuf, dsbuf, acc, sbuf, xbuf, tbuf, rbuf, dqbuf,
+    docsem, lsem, qsend, qrecv, kvsend, kvrecv, relsend, xsend, xrecv, gsend, grecv, dqsend, dqrecv, dqloc,
 ):
     me = lax.axis_index("ctx")
     sec = lax.axis_index("section")
@@ -103,23 +103,61 @@
             for step in range(1, depth):
                 pl.when(relays(step))(lambda: relay_copy(h, step, w).start())
 
-    def g_copy(h, slot, t):
+    def x_copy(h, slot, t):
+        to = lax.rem(sec + t, sections)
+        return pltpu.make_async_remote_copy(
+            src_ref=sbuf.at[h, slot, :, pl.ds(pl.multiple_of(to * piece, piece), piece)],
+            dst_ref=xbuf.at[h, slot, t - 1],
+            send_sem=xsend.at[h, slot, t - 1], recv_sem=xrecv.at[h, slot, t - 1],
+            device_id=dev(me, to), device_id_type=MESH,
+        )
+
+    def g_copy(h, slot):
         d = (reach + 1 - slot) // 2
-        owner_core = (slot - reach) % 2
-        to = lax.rem(sec + t, sections)
-        return pltpu.make_async_remote_copy(
-            src_ref=sbuf.at[h, slot, :, pl.ds(pl.multiple_of(to * piece, piece), piece)],
-            dst_ref=rbuf.at[d, sec, core, h],
-            send_sem=gsend.at[h, slot, t], recv_sem=grecv.at[d, sec, core, h],
-            device_id=dev(2 * (chip - d) + owner_core, to), device_id_type=MESH,
-        )
-
-    def g_wait(h, d, s, c):
-        return pltpu.make_async_remote_copy(
-            src_ref=sbuf.at[h, 0, :, pl.ds(0, piece)], dst_ref=rbuf.at[d, s, c, h],
-            send_sem=gsend.at[h, 0, 0], recv_sem=grecv.at[d, s, c, h],
+        return pltpu.make_async_remote_copy(
+            src_ref=tbuf.at[h, slot], dst_ref=rbuf.at[d, core, h],
+            send_sem=gsend.at[h, slot], recv_sem=grecv.at[d, core, h],
+            device_id=dev(2 * (chip - d) + (slot - reach) % 2, sec), device_id_type=MESH,
+        )
+
+    def g_wait(h, d, c):
+        return pltpu.make_async_remote_copy(
+            src_ref=tbuf.at[h, 0], dst_ref=rbuf.at[d, c, h],
+            send_sem=gsend.at[h, 0], recv_sem=grecv.at[d, c, h],
             device_id=dev(2 * chip + other, sec), device_id_type=MESH,
         )
+
+    def when_block(slot, run):
+        if slot < reach:
+            pl.when(2 * chip - reach + slot >= 0)(run)
+        else:
+            run()
+
+    def when_sent(slot, run):
+        pl.when(2 * chip - reach + slot >= 0 if slot < reach else core != slot - reach)(run)
+
+    def scatter(h):
+        def send(slot):
+            for t in range(1, sections):
+                x_copy(h, slot, t).start()
+
+        for slot in range(blocks):
+            when_block(slot, functools.partial(send, slot))
+
+    def deliver(h):
+        own = pl.ds(pl.multiple_of(sec * piece, piece), piece)
+
+        def run(slot):
+            total = sbuf[h, slot, :, own].astype(jnp.float32)
+            for t in range(1, sections):
+                x_copy(h, slot, t).wait_recv()
+                total = total + xbuf[h, slot, t - 1].astype(jnp.float32)
+            tbuf[h, slot] = total.astype(jnp.bfloat16)
+            when_sent(slot, lambda: g_copy(h, slot).start())
+
+        for slot in range(blocks):
+            when_block(slot, functools.partial(run, slot))
+        rbuf[0, core, h] = tbuf[h, reach + core]
 
     def dq_copy(h):
         return pltpu.make_async_remote_copy(
@@ -274,20 +312,12 @@
             at = slice(slot * rows, (slot + 1) * rows)
             sbuf[h, slot, 0] = (acc[0, at] * scale).astype(jnp.bfloat16)
             sbuf[h, slot, 1] = acc[1, at].astype(jnp.bfloat16)
-        own = pl.ds(pl.multiple_of(sec * piece, piece), piece)
-        rbuf[0, sec, core, h] = sbuf[h, reach + core, :, own]
-        for slot in range(blocks):
-            for t in range(sections):
-                if slot < reach:
-                    condition = 2 * chip - reach + slot >= 0
-                elif t == 0:
-                    condition = core != slot - reach
-                else:
-                    condition = None
-                if condition is None:
-                    g_copy(h, slot, t).start()
-                else:
-                    pl.when(condition)(lambda: g_copy(h, slot, t).start())
+        scatter(h)
+
+        @pl.when(h > 0)
+        def _():
+            deliver(h - 1)
+
         return unused
 
     lax.fori_loop(0, heads, head_step, 0)
@@ -301,25 +331,15 @@
 
     lax.fori_loop(0, heads, query_step, 0)
 
+    deliver(heads - 1)
+
     for h in range(heads):
-        for d in range(depth + 1):
-            for s in range(sections):
-                for c in range(2):
-                    if d == 0:
-                        condition = (sec != s) | (core != c)
-                    else:
-                        condition = chip + d < chips
-
-                    @pl.when(condition)
-                    def _():
-                        g_wait(h, d, s, c).wait_recv()
-    for c in range(2):
-        for h in range(heads):
-            total = None
-            for d in range(depth + 1):
-                for s in range(sections):
-                    term = rbuf[d, s, c, h].astype(jnp.float32)
-                    total = term if total is None else total + term
+        for c in range(2):
+            for d in range(depth, -1, -1):
+                pl.when(core != c if d == 0 else chip + d < chips)(lambda: g_wait(h, d, c).wait_recv())
+            total = rbuf[0, c, h].astype(jnp.float32)
+            for d in range(1, depth + 1):
+                total = total + rbuf[d, c, h].astype(jnp.float32)
             g = c * heads + h
             out_ref[:, :, g * HD : (g + 1) * HD] = total.astype(jnp.bfloat16)
 
@@ -338,18 +358,13 @@
         for step in range(1, depth):
             for w in range(2):
                 pl.when(relays(step))(lambda: relay_copy(h, step, w).wait_send())
+        def sent(slot):
+            for t in range(1, sections):
+                x_copy(h, slot, t).wait_send()
+
         for slot in range(blocks):
-            for t in range(sections):
-                if slot < reach:
-                    condition = 2 * chip - reach + slot >= 0
-                elif t == 0:
-                    condition = core != slot - reach
-                else:
-                    condition = None
-                if condition is None:
-                    g_copy(h, slot, t).wait_send()
-                else:
-                    pl.when(condition)(lambda: g_copy(h, slot, t).wait_send())
+            when_block(slot, functools.partial(sent, slot))
+            when_sent(slot, lambda: g_copy(h, slot).wait_send())
         return unused
 
     lax.fori_loop(0, heads, finish, 0)
@@ -390,7 +405,9 @@
             pltpu.VMEM((heads, 2, window, group * layers * rows), bf),
             pltpu.VMEM((2, blocks * rows, HD), f32),
             pltpu.VMEM((heads, blocks, 2, rows, HD), bf),
-            pltpu.VMEM((depth + 1, sections, 2, heads, 2, piece, HD), bf),
+            pltpu.VMEM((heads, blocks, max(sections - 1, 1), 2, piece, HD), bf),
+            pltpu.VMEM((heads, blocks, 2, piece, HD), bf),
+            pltpu.VMEM((depth + 1, 2, heads, 2, piece, HD), bf),
             pltpu.VMEM((heads, 2, layers * rows, group * HD), bf),
             dma,
             dma((heads, 3)),
@@ -399,19 +416,26 @@
             dma((heads, depth + 1, 2)),
             dma((heads, blocks)),
             dma((heads, max(depth - 1, 1), 2)),
-            dma((heads, blocks, sections)),
-            dma((depth + 1, sections, 2, heads)),
+            dma((heads, blocks, max(sections - 1, 1))),
+            dma((heads, blocks, max(sections - 1, 1))),
+            dma((heads, blocks)),
+            dma((depth + 1, 2, heads)),
             dma((heads,)),
             dma((heads,)),
             dma((heads,)),
         ],
         compiler_params=pltpu.CompilerParams(
-            collective_id=0, has_side_effects=True, vmem_limit_bytes=67043328
+            collective_id=0, has_side_effects=True, vmem_limit_bytes=40 * 1024 * 1024
         ),
         name="cross_backward",
     )(
-        queries.reshape(layers * rows, width), grad_out.reshape(layers * rows, width),
-        keys_values, doc_ids.reshape(n, rows),
+        *[
+            pltpu.with_memory_space_constraint(x, pltpu.HBM)
+            for x in (
+                queries.reshape(layers * rows, width), grad_out.reshape(layers * rows, width),
+                keys_values, doc_ids.reshape(n, rows),
+            )
+        ]
     )
     return grad_queries.reshape(queries.shape), grad_kv
 

time: 34.7 us -> 32 us (0.922); the launches traced: 34.5 us -> 31.4 us
  Pallas kernels: 31.2 us -> 29.3 us
  local copies, waits for them, and re-layouts: 2.66 us -> 1.49 us
    pallas_call x1, Pallas kernels: 31.2 us -> 29.3 us  [body(): pl.pallas_call(functools.partial(kernel, n, sections, reach, heads_kv, gr...]
    unnamed x4 -> x2, local copies, waits for them, and re-layouts: 2.66 us -> 1.49 us
where the time goes in v4:
time: 32 us; the launch traced here: 31.4 us
  Pallas kernels  29.3 us (92%)
  local copies, waits for them, and re-layouts  1.49 us (5%)
  between operations  0.64 us (2%)
    pallas_call x1, Pallas kernels, body(): pl.pallas_call(functools.partial(kernel, n, sections, reach, heads_kv, gr...  29.3 us
    unnamed x2, local copies, waits for them, and re-layouts  1.49 us

profile of v4, /device:TPU:13, one launch (start us, length us, event | category | flops | bytes accessed | tf_op | source)
XLA Modules:
  0.0 31.4 jit_solution(2687309720620377241)
XLA Ops:
  0.6 29.3 %cross_backward.1 = (bf16[128,2560]{1,0:T(8,128)(2,1)S(1)}, bf16[2,64,512]{2,1,0:T(8,128)(2,1)S(1)}) custom-call(bf16[128,2560]{1,0:T(8,128)(2,1)} %bitcast.5, bf16[128,2560]{1,0:T(8,128)(2,1)} %bitcast.6, bf16[2,128,512]{2,1,0:T(8,128)(2,1)} %kv_ref.1, s32[16,128]{1,0:T(8,128)} %bitcast.7), custom_call_target="tpu_custom_call" | custom-call | tf_op jit(solution)/shard_map/cross_backward/pallas_call | solution.py:390
  30.0 0.8 %copy.8 = bf16[1,128,2560]{2,1,0:T(8,128)(2,1)} copy(bf16[1,128,2560]{2,1,0:T(8,128)(2,1)S(1)} %bitcast.4) | data formatting | bytes 1310720
  30.8 0.7 %copy.9 = bf16[2,64,512]{2,1,0:T(8,128)(2,1)} copy(bf16[2,64,512]{2,1,0:T(8,128)(2,1)S(1)} %get-tuple-element.9) | data formatting | bytes 262144

commit v5 on v4

--- a/solution.py
+++ b/solution.py
@@ -103,12 +103,12 @@
             for step in range(1, depth):
                 pl.when(relays(step))(lambda: relay_copy(h, step, w).start())
 
-    def x_copy(h, slot, t):
+    def x_copy(h, slot, t, k):
         to = lax.rem(sec + t, sections)
         return pltpu.make_async_remote_copy(
-            src_ref=sbuf.at[h, slot, :, pl.ds(pl.multiple_of(to * piece, piece), piece)],
-            dst_ref=xbuf.at[h, slot, t - 1],
-            send_sem=xsend.at[h, slot, t - 1], recv_sem=xrecv.at[h, slot, t - 1],
+            src_ref=sbuf.at[h, slot, k, pl.ds(pl.multiple_of(to * piece, piece), piece)],
+            dst_ref=xbuf.at[h, slot, t - 1, k],
+            send_sem=xsend.at[h, slot, t - 1, k], recv_sem=xrecv.at[h, slot, t - 1, k],
             device_id=dev(me, to), device_id_type=MESH,
         )
 
@@ -136,12 +136,12 @@
     def when_sent(slot, run):
         pl.when(2 * chip - reach + slot >= 0 if slot < reach else core != slot - reach)(run)
 
-    def scatter(h):
+    def scatter(h, k, slots):
         def send(slot):
             for t in range(1, sections):
-                x_copy(h, slot, t).start()
-
-        for slot in range(blocks):
+                x_copy(h, slot, t, k).start()
+
+        for slot in slots:
             when_block(slot, functools.partial(send, slot))
 
     def deliver(h):
@@ -150,7 +150,8 @@
         def run(slot):
             total = sbuf[h, slot, :, own].astype(jnp.float32)
             for t in range(1, sections):
-                x_copy(h, slot, t).wait_recv()
+                for k in range(2):
+                    x_copy(h, slot, t, k).wait_recv()
                 total = total + xbuf[h, slot, t - 1].astype(jnp.float32)
             tbuf[h, slot] = total.astype(jnp.bfloat16)
             when_sent(slot, lambda: g_copy(h, slot).start())
@@ -260,16 +261,20 @@
             delta = jnp.sum(e * dp, axis=0, keepdims=True) * inverse
             p = (e * inverse).astype(jnp.bfloat16)
             to = slice(i * layers * rows, (i + 1) * layers * rows)
-            pbuf[:, to] = p
+            pbuf[sub, :, to] = p
             dsbuf[h, sub, :, to] = (p.astype(jnp.float32) * (dp - delta)).astype(jnp.bfloat16)
 
-    def key_part(h, sub):
-        keys_at = pl.ds(pl.multiple_of(sub * rows, rows), window)
-        for k, (weights, buf) in enumerate([(dsbuf.at[h, sub], qbuf), (pbuf, dobuf)]):
+    def key_part(h, k):
+        for sub in (core, other):
+            keys_at = pl.ds(pl.multiple_of(sub * rows, rows), window)
+            weights, buf = ((dsbuf.at[h, sub], qbuf), (pbuf.at[sub], dobuf))[k]
             stack = jnp.concatenate(
                 [buf[h, sub, :, i * HD : (i + 1) * HD] for i in range(group)], axis=0
             )
             acc[k, keys_at] += jnp.dot(weights[...], stack, preferred_element_type=jnp.float32)
+        for slot in range(blocks):
+            total = acc[k, slot * rows : (slot + 1) * rows]
+            sbuf[h, slot, k] = (total * scale if k == 0 else total).astype(jnp.bfloat16)
 
     def query_part(h, sub):
         kt = jnp.transpose(kvbuf[h, 0, pl.ds(sub, reach + 1)].reshape(window, HD))
@@ -298,7 +303,6 @@
         for copy in local_copies(h)[:2]:
             copy.wait()
         score_part(h, core)
-        key_part(h, core)
 
         @pl.when(h + 1 < heads)
         def _():
@@ -307,17 +311,12 @@
         for copy in q_copies(h):
             copy.wait_recv()
         score_part(h, other)
-        key_part(h, other)
-        for slot in range(blocks):
-            at = slice(slot * rows, (slot + 1) * rows)
-            sbuf[h, slot, 0] = (acc[0, at] * scale).astype(jnp.bfloat16)
-            sbuf[h, slot, 1] = acc[1, at].astype(jnp.bfloat16)
-        scatter(h)
-
-        @pl.when(h > 0)
-        def _():
-            deliver(h - 1)
-
+        key_part(h, 1)
+        scatter(h, 1, range(reach))
+        key_part(h, 0)
+        scatter(h, 0, range(reach))
+        for k in range(2):
+            scatter(h, k, range(reach, blocks))
         return unused
 
     lax.fori_loop(0, heads, head_step, 0)
@@ -327,11 +326,10 @@
         dq_copy(h).start()
         query_part(h, core)
         dq_local(h).start()
+        deliver(h)
         return unused
 
     lax.fori_loop(0, heads, query_step, 0)
-
-    deliver(heads - 1)
 
     for h in range(heads):
         for c in range(2):
@@ -360,7 +358,8 @@
                 pl.when(relays(step))(lambda: relay_copy(h, step, w).wait_send())
         def sent(slot):
             for t in range(1, sections):
-                x_copy(h, slot, t).wait_send()
+                for k in range(2):
+                    x_copy(h, slot, t, k).wait_send()
 
         for slot in range(blocks):
             when_block(slot, functools.partial(sent, slot))
@@ -401,7 +400,7 @@
             pltpu.VMEM((heads, 2, layers * rows, group * HD), bf),
             pltpu.VMEM((heads, 2, blocks, rows, HD), bf),
             pltpu.VMEM((2, window, rows), f32),
-            pltpu.VMEM((window, group * layers * rows), bf),
+            pltpu.VMEM((2, window, group * layers * rows), bf),
             pltpu.VMEM((heads, 2, window, group * layers * rows), bf),
             pltpu.VMEM((2, blocks * rows, HD), f32),
             pltpu.VMEM((heads, blocks, 2, rows, HD), bf),
@@ -416,8 +415,8 @@
             dma((heads, depth + 1, 2)),
             dma((heads, blocks)),
             dma((heads, max(depth - 1, 1), 2)),
-            dma((heads, blocks, max(sections - 1, 1))),
-            dma((heads, blocks, max(sections - 1, 1))),
+            dma((heads, blocks, max(sections - 1, 1), 2)),
+            dma((heads, blocks, max(sections - 1, 1), 2)),
             dma((heads, blocks)),
             dma((depth + 1, 2, heads)),
             dma((heads,)),

time: 32 us -> 31.7 us (level); the launches traced: 31.4 us -> 31.6 us
  no operation moved by 1% of the time
where the time goes in v5:
time: 31.7 us; the launch traced here: 31.6 us
  Pallas kernels  29.4 us (93%)
  local copies, waits for them, and re-layouts  1.49 us (5%)
  between operations  0.64 us (2%)
    pallas_call x1, Pallas kernels, body(): pl.pallas_call(functools.partial(kernel, n, sections, reach, heads_kv, gr...  29.4 us
    unnamed x2, local copies, waits for them, and re-layouts  1.49 us

profile of v5, /device:TPU:13, one launch (start us, length us, event | category | flops | bytes accessed | tf_op | source)
XLA Modules:
  0.0 31.6 jit_solution(2815740845539217093)
XLA Ops:
  0.6 29.4 %cross_backward.1 = (bf16[128,2560]{1,0:T(8,128)(2,1)S(1)}, bf16[2,64,512]{2,1,0:T(8,128)(2,1)S(1)}) custom-call(bf16[128,2560]{1,0:T(8,128)(2,1)} %bitcast.5, bf16[128,2560]{1,0:T(8,128)(2,1)} %bitcast.6, bf16[2,128,512]{2,1,0:T(8,128)(2,1)} %kv_ref.1, s32[16,128]{1,0:T(8,128)} %bitcast.7), custom_call_target="tpu_custom_call" | custom-call | tf_op jit(solution)/shard_map/cross_backward/pallas_call | solution.py:389
  30.1 0.8 %copy.8 = bf16[1,128,2560]{2,1,0:T(8,128)(2,1)} copy(bf16[1,128,2560]{2,1,0:T(8,128)(2,1)S(1)} %bitcast.4) | data formatting | bytes 1310720
  30.9 0.7 %copy.9 = bf16[2,64,512]{2,1,0:T(8,128)(2,1)} copy(bf16[2,64,512]{2,1,0:T(8,128)(2,1)S(1)} %get-tuple-element.9) | data formatting | bytes 262144
